TPU v7x, 256 devices: a whole 4x4x8 slice. The times are simulated.
256 devices in a mesh: comp: 2 (over x_lo), ox: 16 (over x_hi, y, core), oy: 8 (over z).
Axes of the slice: x: 4 (x_hi: 2, x_lo: 2; x = x_hi * 2 + x_lo), y: 4, z: 8, core: 2. Of those that a mesh axis runs over, the one named last changes fastest.
Arguments:
- atmos_stress: float32 [2, 2359296], P(None, ('comp', 'ox', 'oy')), may hold values from -6 to 6
- route_tile: int32 [2359296, 1], P(('comp', 'ox', 'oy')), may hold values from 0 to 255; in each aligned block of 9216 rows (0 to 9215, 9216 to 18431, ...) at most 144 rows name the same one
- route_cell: int32 [2359296], P(('comp', 'ox', 'oy')), may hold values from 0 to 54674
- route_weight: float32 [2359296], P(('comp', 'ox', 'oy')), may hold values from 0.25 to 1
- velocity: float32 [2, 8, 4320, 3240], P(None, None, ('comp', 'ox'), 'oy'), may hold values from -6 to 6
- thickness: float32 [8, 4320, 3240], P(None, ('comp', 'ox'), 'oy'), may hold values from 0.5 to 2
- coriolis: float32 [4320, 3240], P(('comp', 'ox'), 'oy'), may hold values from -0.5 to 0.5
- ocean_axes: float32 [2, 3, 4320, 3240], P(None, None, ('comp', 'ox'), 'oy'), may hold values from -3 to 3
- ocean_mask: int32 [4320, 3240], P(('comp', 'ox'), 'oy'), may hold values 0 or 1
Outputs:
- new_velocity: float32 [2, 8, 4320, 3240], P(None, None, ('comp', 'ox'), 'oy')
Inputs may be any that keep to these rules, and one draw needn't show every extreme that they name: `route_tile`: tiles are numbered as devices, comp-major, then ox, then oy. Of the 9216 cells of one device, at most 144 name the same tile, and on some device exactly 144 do.
All inputs are finite; a program needn't handle non-finite values. No bound on the sum of `ocean_mask` on one device may be relied on, other than what follows from the above.
Results may differ from a plain program's by a relative error of at most 0.0003.
Values sent between devices are 32-bit elements; how exact they have to be, the bound alone decides.
A program may use at most 128 MiB of HBM per device.

v0:
```python
import math
import jax
import jax.numpy as jnp
import numpy as np
from jax import lax
from jax.sharding import PartitionSpec as P

A_ROWS = 48
A_COLS = 64
face_normal = np.array(
    [[1.0, 0, 0], [0, 1.0, 0], [-1.0, 0, 0], [0, -1.0, 0], [0, 0, 1.0], [0, 0, -1.0]]
)
face_first = np.array(
    [[0, 1.0, 0], [-1.0, 0, 0], [0, -1.0, 0], [1.0, 0, 0], [0, 1.0, 0], [0, 1.0, 0]]
)
face_second = np.array(
    [[0, 0, 1.0], [0, 0, 1.0], [0, 0, 1.0], [0, 0, 1.0], [-1.0, 0, 0], [1.0, 0, 0]]
)
viscosity = 0.2
coupling = 0.3
bottom_drag = 0.1


def extended(block, sides, width, periodic):
    for axis, dim in sides:
        count = lax.axis_size(axis)
        forward = [(i, i + 1) for i in range(count - 1)]
        if periodic:
            forward.append((count - 1, 0))
        backward = [(target, source) for source, target in forward]
        low = lax.ppermute(
            lax.slice_in_dim(block, block.shape[dim] - width, None, axis=dim), axis, forward
        )
        high = lax.ppermute(lax.slice_in_dim(block, 0, width, axis=dim), axis, backward)
        block = jnp.concatenate([low, block, high], axis=dim)
    return block


def frame_rows(face_table, face_id):
    face_numbers = jnp.arange(6, dtype=jnp.int32)
    face_hits = (face_id[None, :] == face_numbers[:, None]).astype(jnp.float32)
    return jnp.dot(
        jnp.asarray(face_table.T, dtype=jnp.float32), face_hits, precision=lax.Precision.HIGHEST
    )


def tangent(direction, radial):
    projected = direction - jnp.sum(direction * radial, axis=0, keepdims=True) * radial
    return projected / jnp.sqrt(jnp.sum(projected * projected, axis=0, keepdims=True))


def cartesian(stress, face_id, cell_row, cell_col, cube_rows, cube_cols):
    normal = frame_rows(face_normal, face_id)
    first_axis = frame_rows(face_first, face_id)
    second_axis = frame_rows(face_second, face_id)
    slant_row = jnp.tan(
        (cell_row.astype(jnp.float32) + 0.5) * (0.5 * math.pi / cube_rows) - 0.25 * math.pi
    )
    slant_col = jnp.tan(
        (cell_col.astype(jnp.float32) + 0.5) * (0.5 * math.pi / cube_cols) - 0.25 * math.pi
    )
    surface_point = normal + slant_row[None, :] * first_axis + slant_col[None, :] * second_axis
    radial = surface_point / jnp.sqrt(jnp.sum(surface_point * surface_point, axis=0, keepdims=True))
    return stress[0][None, :] * tangent(first_axis, radial) + stress[1][None, :] * tangent(
        second_axis, radial
    )


def advance(masked, east, west, north, south, thickness, coriolis, ocean_stress, sea_mask):
    laplacian = east + west + north + south - 4.0 * masked
    turning = jnp.stack([coriolis * masked[1], -coriolis * masked[0]])
    interface_depth = 0.5 * (thickness[:-1] + thickness[1:])
    inner_flux = coupling * (masked[:, :-1] - masked[:, 1:]) / interface_depth[None]
    fluxes = jnp.concatenate(
        [ocean_stress[:, None], inner_flux, bottom_drag * masked[:, -1:]], axis=1
    )
    vertical = (fluxes[:, :-1] - fluxes[:, 1:]) / thickness[None]
    return (masked + turning + viscosity * laplacian + vertical) * sea_mask


def pack_blocks(payload, target, tile_count, capacity):
    cell_count = target.shape[0]
    block_len = math.gcd(cell_count, 512)
    block_count = cell_count // block_len
    tile_numbers = jnp.arange(tile_count, dtype=jnp.int32)
    hits = (target[:, None] == tile_numbers[None, :]).astype(jnp.float32)
    hit_blocks = hits.reshape(block_count, block_len, tile_count)
    lower = (jnp.arange(block_len)[:, None] > jnp.arange(block_len)[None, :]).astype(jnp.bfloat16)
    within = jnp.einsum(
        "ij,bjt->bit", lower, hit_blocks.astype(jnp.bfloat16), preferred_element_type=jnp.float32
    )
    totals = jnp.sum(hit_blocks, axis=1)
    before = jnp.cumsum(totals, axis=0) - totals
    rank_blocks = jnp.sum((within + before[:, None, :]) * hit_blocks, axis=2)
    payload_blocks = payload.reshape(payload.shape[0], block_count, block_len).transpose(1, 0, 2)
    slot_numbers = jnp.arange(capacity, dtype=jnp.float32)

    def pack_add_block(packed, pieces):
        hit_block, rank_block, payload_block = pieces
        slot_hits = (rank_block[:, None] == slot_numbers[None, :]).astype(jnp.float32)
        spread = payload_block[:, :, None] * hit_block[None, :, :]
        return (
            packed + jnp.einsum("cgt,gs->cts", spread, slot_hits, precision=lax.Precision.HIGHEST),
            None,
        )

    start = jnp.zeros((payload.shape[0], tile_count, capacity), jnp.float32)
    packed, unused = lax.scan(pack_add_block, start, (hit_blocks, rank_blocks, payload_blocks))
    return packed


def unpack_blocks(received, tile_count, capacity, tile_width, tile_depth):
    group = 1
    while group * 2 <= tile_count and group * 2 * capacity <= 2048:
        group = group * 2
    group_count = tile_count // group
    blocks = received.reshape(4, group_count, group * capacity).transpose(1, 0, 2)
    x_numbers = jnp.arange(tile_width, dtype=jnp.int32)
    y_numbers = jnp.arange(tile_depth, dtype=jnp.int32)

    def unpack_add_block(surface, block):
        cell_number = block[3].astype(jnp.int32)
        x_offset = cell_number // tile_depth
        y_offset = cell_number % tile_depth
        x_hits = (x_offset[None, :] == x_numbers[:, None]).astype(jnp.float32)
        y_hits = (y_offset[:, None] == y_numbers[None, :]).astype(jnp.float32)
        spread = (block[:3][:, None, :] * x_hits[None]).reshape(3 * tile_width, -1)
        return (surface + jnp.dot(spread, y_hits, precision=lax.Precision.HIGHEST), None)

    start = jnp.zeros((3 * tile_width, tile_depth), jnp.float32)
    surface, unused = lax.scan(unpack_add_block, start, blocks)
    return surface.reshape(3, tile_width, tile_depth)


def shards(
    atmos_stress,
    route_tile,
    route_cell,
    route_weight,
    velocity,
    thickness,
    coriolis,
    ocean_axes,
    ocean_mask,
):
    cell_count = atmos_stress.shape[1]
    face_block = A_ROWS * A_COLS
    halves = lax.axis_size("comp")
    rows_axis = lax.axis_size("ox")
    cols_axis = lax.axis_size("oy")
    tile_count = halves * rows_axis * cols_axis
    capacity = 4 * cell_count // tile_count
    local_index = jnp.arange(cell_count, dtype=jnp.int32)
    face_id = lax.axis_index("comp") * (cell_count // face_block) + local_index // face_block
    cell_row = lax.axis_index("ox") * A_ROWS + local_index // A_COLS % A_ROWS
    cell_col = lax.axis_index("oy") * A_COLS + local_index % A_COLS
    weighted = (
        cartesian(atmos_stress, face_id, cell_row, cell_col, A_ROWS * rows_axis, A_COLS * cols_axis)
        * route_weight[None, :]
    )
    target = route_tile[:, 0]
    payload = jnp.concatenate([weighted, route_cell.astype(jnp.float32)[None, :]], axis=0)
    packed = pack_blocks(payload, target, tile_count, capacity)
    packed = packed.reshape(4, halves, rows_axis * cols_axis, capacity)
    received = lax.all_to_all(
        lax.all_to_all(packed, "comp", split_axis=1, concat_axis=1, tiled=True),
        ("ox", "oy"),
        split_axis=2,
        concat_axis=2,
        tiled=True,
    )
    tile_width = velocity.shape[2]
    tile_depth = velocity.shape[3]
    surface = unpack_blocks(received.reshape(4, -1), tile_count, capacity, tile_width, tile_depth)
    ocean_stress = jnp.sum(ocean_axes * surface[None], axis=1)
    sea_mask = ocean_mask.astype(jnp.float32)
    masked = velocity * sea_mask
    x_rims = extended(masked, ((("comp", "ox"), 2),), 1, True)
    y_rims = extended(masked, (("oy", 3),), 1, False)
    top_row = masked[:, :, :, -1]
    position = lax.axis_index("comp") * rows_axis + lax.axis_index("ox")
    whole_row = lax.all_gather(top_row, ("comp", "ox"), axis=2, tiled=True)
    mirrored = whole_row[:, :, ::-1]
    folded = lax.dynamic_slice_in_dim(mirrored, position * tile_width, tile_width, 2)
    at_fold = lax.axis_index("oy") == cols_axis - 1
    north_rim = jnp.where(at_fold, -folded, y_rims[:, :, :, -1])
    east = x_rims[:, :, 2:, :]
    west = x_rims[:, :, :-2, :]
    north = jnp.concatenate([y_rims[:, :, :, 2:-1], north_rim[:, :, :, None]], axis=3)
    south = y_rims[:, :, :, :-2]
    return advance(masked, east, west, north, south, thickness, coriolis, ocean_stress, sea_mask)


def solution(mesh):
    return jax.shard_map(
        shards,
        mesh=mesh,
        in_specs=(
            P(None, ("comp", "ox", "oy")),
            P(("comp", "ox", "oy"), None),
            P(("comp", "ox", "oy")),
            P(("comp", "ox", "oy")),
            P(None, None, ("comp", "ox"), "oy"),
            P(None, ("comp", "ox"), "oy"),
            P(("comp", "ox"), "oy"),
            P(None, None, ("comp", "ox"), "oy"),
            P(("comp", "ox"), "oy"),
        ),
        out_specs=P(None, None, ("comp", "ox"), "oy"),
        check_vma=False,
    )
```

profile of v0, /device:TPU:1, one launch (start us, length us, event | category | flops | bytes accessed | tf_op | source)
XLA Modules:
  0.0 483.1 jit_solution(10987998646943046107)
XLA Ops:
  3.1 4.8 %fusion.23 = f32[18,512,256]{1,2,0:T(8,128)} fusion(s32[18,512]{1,0:T(8,128)S(1)} %eq.115), kind=kLoop, calls=%fused_computation.36 | loop fusion | flops 4718592 | bytes 9474048 | tf_op jit(solution)/shard_map/convert_element_type | solution.py:86
  9.9 3.8 fusion.22
  14.1 45.8 %while.24 = (s32[]{:T(128)}, f32[4,256,144]{1,2,0:T(8,128)S(1)}, f32[18,4,512]{2,1,0:T(4,128)S(1)}, f32[18,512,256]{1,2,0:T(8,128)}, f32[18,512]{1,0:T(8,128)S(1)}, /*index=5*/s32[]{:T(128)}, s32[]{:T(128)}) while((s32[]{:T(128)}, f32[4,256,144]{1,2,0:T(8,128)S(1)}, f32[18,4,512]{2,1,0:T(4,128)S(1)}, f32[18,512,256]{1,2,0:T(8,128)}, ...), condition=%wide.region_9.10_spmd.clone, body=%wide.region_8.9_spmd.clone.sunk | while | flops 906862592 | bytes 3831907 | solution.py:108
  64.5 8.8 %copy.50 = f32[2,8,135,405]{2,1,0,3:T(8,128)} copy(f32[2,8,135,405]{3,1,2,0:T(8,128)} %param.20) | data formatting | bytes 6998400 | tf_op args[4]
  73.3 3.9 broadcast_multiply_fusion.1
  79.1 5.6 %collective-permute-start.3 = (f32[2,8,135,1]{2,1,0,3:T(8,128)S(1)}, f32[2,8,135,1]{2,1,0,3:T(8,128)}, u32[]{:S(2)}, u32[]{:S(2)}) collective-permute-start(f32[2,8,135,1]{2,1,0,3:T(8,128)S(1)} %get-tuple-element.195), channel_id=1, source_target_pairs={{0,1},{1,2},{2,3},{3,4},{4,5},{5,6},{6,7},{8,9},{9,10},{10,11},{11... | collective-permute-start | bytes 25928 | tf_op jit(solution)/shard_map/ppermute | solution.py:31
  84.7 4.0 fusion.75
  99.1 4.7 copy.66
  103.8 9.4 %fusion.27 = f32[2,7,135,405]{2,1,0,3:T(8,128)} fusion(f32[2,8,135,405]{2,1,0,3:T(8,128)} %copy-done, f32[7,135,405]{1,0,2:T(8,128)} %copy.66), kind=kLoop, calls=%fused_computation.41 | loop fusion | flops 2296350 | bytes 10716300 | tf_op jit(solution)/shard_map/div | solution.py:73
  116.4 15.2 %all-to-all-start.1 = ((f32[4,2,128,144]{3,1,0,2:T(2,128)}), f32[4,2,128,144]{3,1,0,2:T(2,128)S(1)}, u32[]{:S(2)}, u32[]{:S(2)}) async-start(f32[4,2,128,144]{3,1,0,2:T(2,128)} %copy.62), calls=%async_computation.1 | async-start | bytes 2097152 | tf_op jit(solution)/shard_map/all_to_all | solution.py:165
  131.5 6.5 %slice_multiply_fusion.1 = (f32[1,8,135,405]{2,1,0,3:T(8,128)}, f32[1,8,135,405]{2,1,0,3:T(8,128)}) fusion(f32[2,8,135,405]{2,1,0,3:T(8,128)} %copy-done, f32[135,405]{0,1:T(8,128)} %copy.51, f32[135,405]{0,1:T(8,128)} %copy.52), kind=kLoop, calls=%fused_computation.59 | loop fusion | flops 874800 | bytes 7435800 | tf_op jit(solution)/shard_map/mul | solution.py:71
  138.2 4.8 slice_multiply_fusion.2
  143.0 62.0 %all-gather = f32[2,8,4320,1]{1,0,3,2:T(2,128)} all-gather(f32[2,8,135,1]{1,0,3,2:T(2,128)S(1)} %copy.57), channel_id=2, replica_groups=mesh['comp'=2,'ox'=16,'oy'=8] {'comp','ox'}, dimensions={2}, use_global_device_ids=true | all-gather | bytes 285120 | tf_op jit(solution)/shard_map/all_gather | solution.py:182
  204.9 6.4 %slice.95 = f32[2,8,135,404]{2,1,0,3:T(8,128)} slice(f32[2,8,135,405]{2,1,0,3:T(8,128)} %copy-done), slice={[0:2], [0:8], [0:135], [1:405]} | slice | bytes 6981120 | tf_op jit(solution)/shard_map/slice | solution.py:189
  214.6 5.2 %copy.58 = f32[2,8,4320,1]{2,1,0,3:T(8,128)S(1)} copy(f32[2,8,4320,1]{1,0,3,2:T(2,128)} %all-gather) | data formatting | bytes 552960 | tf_op jit(solution)/shard_map/all_gather | solution.py:182
  229.0 206.2 %while.25 = (s32[]{:T(128)}, f32[405,405]{1,0:T(8,128)}, f32[32,4,1152]{2,0,1:T(8,128)S(1)}, s32[]{:T(128)}, s32[]{:T(128)}, /*index=5*/s32[]{}) while((s32[]{:T(128)}, f32[405,405]{1,0:T(8,128)}, f32[32,4,1152]{2,0,1:T(8,128)S(1)}, s32[]{:T(128)}, s32[]{:T(128)}, /*index=5*/s32[]{}) %tuple.73), condition=%wide.region_11.12_spmd.clone, body=%wide.region_10.11_spmd.clone.sunk | while | flops 2269070080 | bytes 15387791 | solution.py:131
  237.3 3.7 fusion.93
  250.2 3.7 fusion.93
  263.1 3.7 fusion.93
  276.0 3.7 fusion.93
  301.7 3.7 fusion.93
  437.5 4.1 multiply_reduce_fusion
  445.0 29.2 %fusion.33 = f32[2,8,135,405]{2,1,0,3:T(8,128)} fusion(f32[2,8,135,405]{2,1,0,3:T(8,128)} %copy-done, f32[2,8,135,1]{2,1,0,3:T(8,128)} %collective-permute-done.3, f32[2,8,1,405]{2,1,0,3:T(8,128)} %copy.56, f32[2,8,1,405]{2,1,0,3:T(8,128)S(1)} %copy-done.2, f32[1,8,135,405]{2,1,0,3:T(8,128)} %get-tuple-element.197, ...), kind=kLoop, calls=%fused_computation.48 | loop fusion | flops 16621200 | bytes 19962180 | tf_op jit(solution)/shard_map/mul | solution.py:78
  474.2 8.8 %copy.69 = f32[2,8,135,405]{3,1,2,0:T(8,128)} copy(f32[2,8,135,405]{2,1,0,3:T(8,128)} %fusion.33) | data formatting | bytes 6998400 | tf_op jit(solution)/shard_map/mul | solution.py:78
  (580 shorter events, 273.9 us)
Async XLA Ops:
  0.0 7.9 %copy-start.13 = (f32[3,6]{1,0:T(4,128)S(1)}, f32[3,6]{1,0:T(4,128)}, u32[]{:S(2)}) copy-start(f32[3,6]{1,0:T(4,128)} %constant.156.clone) | copy-start | bytes 220
  0.0 8.2 %copy-start.12 = (f32[3,6]{1,0:T(4,128)S(1)}, f32[3,6]{1,0:T(4,128)}, u32[]{:S(2)}) copy-start(f32[3,6]{1,0:T(4,128)} %constant.155.clone) | copy-start | bytes 220
  0.0 8.8 %copy-start.11 = (f32[3,6]{1,0:T(4,128)S(1)}, f32[3,6]{1,0:T(4,128)}, u32[]{:S(2)}) copy-start(f32[3,6]{1,0:T(4,128)} %constant.154.clone) | copy-start | bytes 220
  0.0 9.8 %copy-start.8 = (f32[2,9216]{1,0:T(2,128)S(1)}, f32[2,9216]{1,0:T(2,128)}, u32[]{:S(2)}) copy-start(f32[2,9216]{1,0:T(2,128)} %param.16) | copy-start | bytes 221188
  0.0 9.8 %copy-start.10 = (s32[9216]{0:T(1024)S(1)}, s32[9216]{0:T(1024)}, u32[]{:S(2)}) copy-start(s32[9216]{0:T(1024)} %param.18) | copy-start | bytes 110596
  9.9 3.9 copy-start.9
  14.1 50.2 %copy-start.7 = (s32[135,405]{1,0:T(8,128)S(1)}, s32[135,405]{1,0:T(8,128)}, u32[]{:S(2)}) copy-start(s32[135,405]{1,0:T(8,128)} %param.24) | copy-start | bytes 656104
  60.8 54.3 %all-to-all-start = ((f32[4,2,128,144]{2,3,0,1:T(8,128)}), f32[4,2,128,144]{2,3,0,1:T(8,128)S(1)}, u32[]{:S(2)}, u32[]{:S(2)}) async-start(f32[4,2,128,144]{2,3,0,1:T(8,128)} %copy_bitcast_fusion.1), calls=%async_computation | async-start | bytes 1179648 | tf_op jit(solution)/shard_map/all_to_all | solution.py:166
  64.5 12.7 %copy-start.3 = (f32[135,405]{0,1:T(8,128)}, f32[135,405]{0,1:T(8,128)S(1)}, u32[]{:S(2)}) copy-start(f32[135,405]{0,1:T(8,128)S(1)} %copy.49) | copy-start | bytes 656104
  77.2 11.5 %copy-start = (f32[2,8,135,405]{2,1,0,3:T(8,128)}, f32[2,8,135,405]{2,1,0,3:T(8,128)S(1)}, u32[]{:S(2)}) copy-start(f32[2,8,135,405]{2,1,0,3:T(8,128)S(1)} %broadcast_multiply_fusion.1) | copy-start | bytes 10497604
  77.9 144.6 %collective-permute-start.2 = (f32[2,8,135,1]{2,1,0,3:T(8,128)}, f32[2,8,135,1]{2,1,0,3:T(8,128)}, u32[]{:S(2)}, u32[]{:S(2)}) collective-permute-start(f32[2,8,135,1]{2,1,0,3:T(8,128)} %get-tuple-element.194), channel_id=1, source_target_pairs={{1,0},{2,1},{3,2},{4,3},{5,4},{6,5},{7,6},{9,8},{10,9},{11,10},{12... | collective-permute-start | bytes 25928 | tf_op jit(solution)/shard_map/ppermute | solution.py:34
  79.1 365.9 %collective-permute-start.3 = (f32[2,8,135,1]{2,1,0,3:T(8,128)S(1)}, f32[2,8,135,1]{2,1,0,3:T(8,128)}, u32[]{:S(2)}, u32[]{:S(2)}) collective-permute-start(f32[2,8,135,1]{2,1,0,3:T(8,128)S(1)} %get-tuple-element.195), channel_id=1, source_target_pairs={{0,1},{1,2},{2,3},{3,4},{4,5},{5,6},{6,7},{8,9},{9,10},{10,11},{11... | collective-permute-start | bytes 25928 | tf_op jit(solution)/shard_map/ppermute | solution.py:31
  88.7 8.6 %copy-start.1 = (f32[8,135,405]{2,0,1:T(8,128)S(1)}, f32[8,135,405]{2,0,1:T(8,128)}, u32[]{:S(2)}) copy-start(f32[8,135,405]{2,0,1:T(8,128)} %param.21) | copy-start | bytes 5248804
  91.6 131.6 %collective-permute-start = (f32[2,8,1,405]{3,1,2,0:T(8,128)S(1)}, f32[2,8,1,405]{3,1,2,0:T(8,128)S(1)}, u32[]{:S(2)}, u32[]{:S(2)}) collective-permute-start(f32[2,8,1,405]{3,1,2,0:T(8,128)S(1)} %copy.53), channel_id=1, source_target_pairs={{8,0},{16,8},{24,16},{32,24},{40,32},{48,40},{56,48},{64,56},{72,6... | collective-permute-start | bytes 77768 | tf_op jit(solution)/shard_map/ppermute | solution.py:34
  97.3 128.5 %collective-permute-start.1 = (f32[2,8,1,405]{3,1,2,0:T(8,128)S(1)}, f32[2,8,1,405]{3,1,2,0:T(8,128)S(1)}, u32[]{:S(2)}, u32[]{:S(2)}) collective-permute-start(f32[2,8,1,405]{3,1,2,0:T(8,128)S(1)} %copy.55), channel_id=1, source_target_pairs={{0,8},{8,16},{16,24},{24,32},{32,40},{40,48},{48,56},{56,64},{64,7... | collective-permute-start | bytes 77768 | tf_op jit(solution)/shard_map/ppermute | solution.py:31
  103.8 9.4 %copy-start.4 = (f32[135,405]{1,0:T(8,128)S(1)}, f32[135,405]{1,0:T(8,128)}, u32[]{:S(2)}) copy-start(f32[135,405]{1,0:T(8,128)} %param.22) | copy-start | bytes 656104
  116.4 111.9 %all-to-all-start.1 = ((f32[4,2,128,144]{3,1,0,2:T(2,128)}), f32[4,2,128,144]{3,1,0,2:T(2,128)S(1)}, u32[]{:S(2)}, u32[]{:S(2)}) async-start(f32[4,2,128,144]{3,1,0,2:T(2,128)} %copy.62), calls=%async_computation.1 | async-start | bytes 2097152 | tf_op jit(solution)/shard_map/all_to_all | solution.py:165
  229.1 1.8 copy-start.5
  235.5 1.8 copy-start.5
  242.0 1.8 copy-start.5
  248.4 1.8 copy-start.5
  254.8 1.8 copy-start.5
  261.3 1.8 copy-start.5
  435.2 9.8 %copy-start.2 = (f32[2,8,1,405]{2,1,0,3:T(8,128)S(1)}, f32[2,8,1,405]{2,1,0,3:T(8,128)}, u32[]{:S(2)}) copy-start(f32[2,8,1,405]{2,1,0,3:T(8,128)} %copy.54) | copy-start | bytes 77764
  (58 other events, 75.7 us)
where the time goes:
time: 486 us; the launch traced here: 483 us
  local copies, waits for them, and re-layouts  166 us (34%)
  matrix products  145 us (30%)
  other arithmetic  77.8 us (16%)
  blocking collectives  62 us (13%)
  starting transfers between devices  28.6 us (6%)
    dot_general x32, matrix products, unpack_add_block(): jnp.dot(spread, y_hits, precision=lax.Precision.HIGHEST)  119 us
    all_gather x1, blocking collectives, shards(): whole_row = lax.all_gather(top_row, ('comp', 'ox'), axis=2, tiled=True)  62 us
    mul x32, local copies, waits for them, and re-layouts, unpack_add_block(): spread = (block[:3][:, None, :] * x_hits[None]).reshape(3 * tile_width, -1)  46.6 us
    mul x1, other arithmetic, advance(): return (masked + turning + viscosity * laplacian + vertical) * sea_mask  29.2 us
    while x160, local copies, waits for them, and re-layouts  28.7 us
    dynamic_slice x54, local copies, waits for them, and re-layouts, pack_blocks(): lax.scan(pack_add_block, start, (hit_blocks, rank_blocks, payload_blocks))  23.2 us
    dot_general x18, matrix products, pack_add_block(): jnp.einsum('cgt,gs->cts', spread, slot_hits, precision=lax.Precision.HIGH...  21.4 us
    unnamed x30, local copies, waits for them, and re-layouts  16.1 us
  transfers between devices with their start and end apart: 6, of which 0 were waited for; matrix products, arithmetic and copies ran while one was open for 54% of the time, Pallas kernels for 0%

commit v1 on v0

--- a/solution.py
+++ b/solution.py
@@ -179,7 +179,10 @@
     y_rims = extended(masked, (("oy", 3),), 1, False)
     top_row = masked[:, :, :, -1]
     position = lax.axis_index("comp") * rows_axis + lax.axis_index("ox")
-    whole_row = lax.all_gather(top_row, ("comp", "ox"), axis=2, tiled=True)
+    whole_row = jnp.concatenate(
+        lax.all_to_all(jnp.stack([top_row] * lax.axis_size(("comp", "ox"))), ("comp", "ox"), 0, 0),
+        axis=2,
+    )
     mirrored = whole_row[:, :, ::-1]
     folded = lax.dynamic_slice_in_dim(mirrored, position * tile_width, tile_width, 2)
     at_fold = lax.axis_index("oy") == cols_axis - 1

time: 486 us -> 432 us (0.89)
  blocking collectives: 62 us -> 0 us
  starting transfers between devices: 28.6 us -> 37.4 us
    all_gather x1 -> x0, blocking collectives: 62 us -> none  [shards(): whole_row = lax.all_gather(top_row, ('comp', 'ox'), axis=2, tiled=True)]
    all_to_all x0 -> x1, starting transfers between devices: none -> 9.57 us  [shards(): lax.all_to_all(jnp.stack([top_row] * lax.axis_size(('comp', 'ox'))), ('co...]
    all_gather x1 -> x0, local copies, waits for them, and re-layouts: 5.21 us -> none  [shards(): whole_row = lax.all_gather(top_row, ('comp', 'ox'), axis=2, tiled=True)]
    unnamed x30 -> x34, local copies, waits for them, and re-layouts: 16.1 us -> 17.8 us
  transfers between devices with their start and end apart: 6 -> 7, of which waited for: 0 -> 1; matrix products, arithmetic and copies ran while one was open for 54% -> 61% of each run, Pallas kernels for 0% -> 0%
where the time goes in v1:
time: 432 us; the launch traced here: 429 us
  local copies, waits for them, and re-layouts  163 us (38%)
  matrix products  145 us (34%)
  other arithmetic  78 us (18%)
  starting transfers between devices  37.4 us (9%)
    dot_general x32, matrix products, unpack_add_block(): jnp.dot(spread, y_hits, precision=lax.Precision.HIGHEST)  119 us
    mul x32, local copies, waits for them, and re-layouts, unpack_add_block(): spread = (block[:3][:, None, :] * x_hits[None]).reshape(3 * tile_width, -1)  46.6 us
    mul x1, other arithmetic, advance(): return (masked + turning + viscosity * laplacian + vertical) * sea_mask  29.5 us
    while x160, local copies, waits for them, and re-layouts  28.3 us
    dynamic_slice x54, local copies, waits for them, and re-layouts, pack_blocks(): lax.scan(pack_add_block, start, (hit_blocks, rank_blocks, payload_blocks))  23.2 us
    dot_general x18, matrix products, pack_add_block(): jnp.einsum('cgt,gs->cts', spread, slot_hits, precision=lax.Precision.HIGH...  21.4 us
    unnamed x34, local copies, waits for them, and re-layouts  17.8 us
    all_to_all x1, starting transfers between devices, shards(): lax.all_to_all(lax.all_to_all(packed, 'comp', split_axis=1, concat_axis=1...  15 us
  transfers between devices with their start and end apart: 7, of which 1 were waited for; matrix products, arithmetic and copies ran while one was open for 61% of the time, Pallas kernels for 0%

profile of v1, /device:TPU:1, one launch (start us, length us, event | category | flops | bytes accessed | tf_op | source)
XLA Modules:
  0.0 428.7 jit_solution(4166266278203362110)
XLA Ops:
  3.1 4.8 %fusion.23 = f32[18,512,256]{1,2,0:T(8,128)} fusion(s32[18,512]{1,0:T(8,128)S(1)} %eq.115), kind=kLoop, calls=%fused_computation.36 | loop fusion | flops 4718592 | bytes 9474048 | tf_op jit(solution)/shard_map/convert_element_type | solution.py:86
  9.9 3.8 fusion.22
  14.1 45.8 %while.24 = (s32[]{:T(128)}, f32[4,256,144]{1,2,0:T(8,128)S(1)}, f32[18,4,512]{2,1,0:T(4,128)S(1)}, f32[18,512,256]{1,2,0:T(8,128)}, f32[18,512]{1,0:T(8,128)S(1)}, /*index=5*/s32[]{:T(128)}, s32[]{:T(128)}) while((s32[]{:T(128)}, f32[4,256,144]{1,2,0:T(8,128)S(1)}, f32[18,4,512]{2,1,0:T(4,128)S(1)}, f32[18,512,256]{1,2,0:T(8,128)}, ...), condition=%wide.region_9.10_spmd.clone, body=%wide.region_8.9_spmd.clone.sunk | while | flops 906862592 | bytes 3831907 | solution.py:108
  64.5 8.8 %copy.48 = f32[2,8,135,405]{2,1,0,3:T(8,128)} copy(f32[2,8,135,405]{3,1,2,0:T(8,128)} %param.20) | data formatting | bytes 6998400 | tf_op args[4]
  73.2 3.9 broadcast_multiply_fusion.1
  78.5 5.0 %collective-permute-start.3 = (f32[2,8,135,1]{2,1,0,3:T(8,128)S(1)}, f32[2,8,135,1]{2,1,0,3:T(8,128)S(1)}, u32[]{:S(2)}, u32[]{:S(2)}) collective-permute-start(f32[2,8,135,1]{2,1,0,3:T(8,128)S(1)} %get-tuple-element.196), channel_id=1, source_target_pairs={{0,1},{1,2},{2,3},{3,4},{4,5},{5,6},{6,7},{8,9},{9,10},{10,11},{11... | collective-permute-start | bytes 25928 | tf_op jit(solution)/shard_map/ppermute | solution.py:31
  83.5 4.0 fusion.74
  97.9 4.7 %copy.63 = f32[7,135,405]{1,0,2:T(8,128)} copy(f32[7,135,405]{2,0,1:T(8,128)} %add_multiply_fusion) | data formatting | bytes 3061800 | tf_op jit(solution)/shard_map/mul | solution.py:72
  103.4 9.6 %all-to-all-start = ((f32[32,2,8,135]{3,2,1,0:T(8,128)}), f32[32,2,8,135]{3,2,1,0:T(8,128)S(1)}, u32[]{:S(2)}, u32[]{:S(2)}) async-start(f32[32,2,8,135]{3,2,1,0:T(8,128)} %stack.9), calls=%async_computation | async-start | bytes 1048576 | tf_op jit(solution)/shard_map/all_to_all | solution.py:183
  113.0 9.4 %fusion.27 = f32[2,7,135,405]{2,1,0,3:T(8,128)} fusion(f32[2,8,135,405]{2,1,0,3:T(8,128)} %copy-done, f32[7,135,405]{1,0,2:T(8,128)} %copy.63), kind=kLoop, calls=%fused_computation.41 | loop fusion | flops 2296350 | bytes 10716300 | tf_op jit(solution)/shard_map/div | solution.py:73
  129.0 15.0 %all-to-all-start.2 = ((f32[4,2,128,144]{3,1,0,2:T(2,128)}), f32[4,2,128,144]{3,1,0,2:T(2,128)S(1)}, u32[]{:S(2)}, u32[]{:S(2)}) async-start(f32[4,2,128,144]{3,1,0,2:T(2,128)} %copy.59), calls=%async_computation.2 | async-start | bytes 2097152 | tf_op jit(solution)/shard_map/all_to_all | solution.py:165
  144.0 4.8 %slice_multiply_fusion.2 = f32[2,1,135,405]{2,1,0,3:T(1,128)} fusion(f32[2,8,135,405]{2,1,0,3:T(8,128)} %copy-done), kind=kLoop, calls=%fused_computation.65 | loop fusion | flops 109350 | bytes 874800 | tf_op jit(solution)/shard_map/mul | solution.py:75
  148.8 6.5 %slice_multiply_fusion.1 = (f32[1,8,135,405]{2,1,0,3:T(8,128)}, f32[1,8,135,405]{2,1,0,3:T(8,128)}) fusion(f32[2,8,135,405]{2,1,0,3:T(8,128)} %copy-done, f32[135,405]{0,1:T(8,128)} %copy.49, f32[135,405]{0,1:T(8,128)} %copy.50), kind=kLoop, calls=%fused_computation.59 | loop fusion | flops 874800 | bytes 7435800 | tf_op jit(solution)/shard_map/mul | solution.py:71
  155.3 6.4 %slice.95 = f32[2,8,135,404]{2,1,0,3:T(8,128)} slice(f32[2,8,135,405]{2,1,0,3:T(8,128)} %copy-done), slice={[0:2], [0:8], [0:135], [1:405]} | slice | bytes 6981120 | tf_op jit(solution)/shard_map/slice | solution.py:192
  174.9 205.6 %while.25 = (s32[]{:T(128)}, f32[405,405]{1,0:T(8,128)}, f32[32,4,1152]{2,0,1:T(8,128)S(1)}, s32[]{:T(128)}, s32[]{:T(128)}, /*index=5*/s32[]{}) while((s32[]{:T(128)}, f32[405,405]{1,0:T(8,128)}, f32[32,4,1152]{2,0,1:T(8,128)S(1)}, s32[]{:T(128)}, s32[]{:T(128)}, /*index=5*/s32[]{}) %tuple.74), condition=%wide.region_11.12_spmd.clone, body=%wide.region_10.11_spmd.clone.sunk | while | flops 2269070080 | bytes 15387791 | solution.py:131
  176.8 3.7 fusion.92
  183.2 3.7 fusion.92
  189.6 3.7 fusion.92
  221.7 3.7 fusion.92
  305.3 3.7 fusion.92
  343.8 3.7 fusion.92
  382.9 4.1 multiply_reduce_fusion
  390.4 29.5 %fusion.33 = f32[2,8,135,405]{2,1,0,3:T(8,128)} fusion(f32[2,8,135,405]{2,1,0,3:T(8,128)} %copy-done, f32[2,8,135,1]{2,1,0,3:T(8,128)S(1)} %collective-permute-done.3, f32[2,8,1,405]{2,1,0,3:T(8,128)} %copy.54, f32[2,8,1,405]{2,1,0,3:T(8,128)S(1)} %copy-done.2, f32[1,8,135,405]{2,1,0,3:T(8,128)} %get-tuple-element.198, ...), kind=kLoop, calls=%fused_computation.48 | loop fusion | flops 16621200 | bytes 19962180 | tf_op jit(solution)/shard_map/mul | solution.py:78
  419.9 8.8 %copy.66 = f32[2,8,135,405]{3,1,2,0:T(8,128)} copy(f32[2,8,135,405]{2,1,0,3:T(8,128)} %fusion.33) | data formatting | bytes 6998400 | tf_op jit(solution)/shard_map/mul | solution.py:78
  (586 shorter events, 273.9 us)
Async XLA Ops:
  0.0 7.9 %copy-start.15 = (f32[3,6]{1,0:T(4,128)S(1)}, f32[3,6]{1,0:T(4,128)}, u32[]{:S(2)}) copy-start(f32[3,6]{1,0:T(4,128)} %constant.156.clone) | copy-start | bytes 220
  0.0 8.2 %copy-start.14 = (f32[3,6]{1,0:T(4,128)S(1)}, f32[3,6]{1,0:T(4,128)}, u32[]{:S(2)}) copy-start(f32[3,6]{1,0:T(4,128)} %constant.155.clone) | copy-start | bytes 220
  0.0 8.8 %copy-start.13 = (f32[3,6]{1,0:T(4,128)S(1)}, f32[3,6]{1,0:T(4,128)}, u32[]{:S(2)}) copy-start(f32[3,6]{1,0:T(4,128)} %constant.154.clone) | copy-start | bytes 220
  0.0 9.8 %copy-start.10 = (f32[2,9216]{1,0:T(2,128)S(1)}, f32[2,9216]{1,0:T(2,128)}, u32[]{:S(2)}) copy-start(f32[2,9216]{1,0:T(2,128)} %param.16) | copy-start | bytes 221188
  0.0 9.8 %copy-start.12 = (s32[9216]{0:T(1024)S(1)}, s32[9216]{0:T(1024)}, u32[]{:S(2)}) copy-start(s32[9216]{0:T(1024)} %param.18) | copy-start | bytes 110596
  9.9 3.9 copy-start.11
  14.1 50.2 %copy-start.9 = (s32[135,405]{1,0:T(8,128)S(1)}, s32[135,405]{1,0:T(8,128)}, u32[]{:S(2)}) copy-start(s32[135,405]{1,0:T(8,128)} %param.24) | copy-start | bytes 656104
  60.7 41.8 %all-to-all-start.1 = ((f32[4,2,128,144]{2,3,0,1:T(8,128)}), f32[4,2,128,144]{2,3,0,1:T(8,128)S(1)}, u32[]{:S(2)}, u32[]{:S(2)}) async-start(f32[4,2,128,144]{2,3,0,1:T(8,128)} %copy_bitcast_fusion.1), calls=%async_computation.1 | async-start | bytes 1179648 | tf_op jit(solution)/shard_map/all_to_all | solution.py:166
  64.5 12.7 %copy-start.3 = (f32[135,405]{0,1:T(8,128)}, f32[135,405]{0,1:T(8,128)S(1)}, u32[]{:S(2)}) copy-start(f32[135,405]{0,1:T(8,128)S(1)} %copy.47) | copy-start | bytes 656104
  77.1 10.3 %copy-start = (f32[2,8,135,405]{2,1,0,3:T(8,128)}, f32[2,8,135,405]{2,1,0,3:T(8,128)S(1)}, u32[]{:S(2)}) copy-start(f32[2,8,135,405]{2,1,0,3:T(8,128)S(1)} %broadcast_multiply_fusion.1) | copy-start | bytes 10497604
  77.2 96.0 %collective-permute-start.2 = (f32[2,8,135,1]{2,1,0,3:T(8,128)S(1)}, f32[2,8,135,1]{2,1,0,3:T(8,128)S(1)}, u32[]{:S(2)}, u32[]{:S(2)}) collective-permute-start(f32[2,8,135,1]{2,1,0,3:T(8,128)S(1)} %get-tuple-element.195), channel_id=1, source_target_pairs={{1,0},{2,1},{3,2},{4,3},{5,4},{6,5},{7,6},{9,8},{10,9},{11,10},{12... | collective-permute-start | bytes 25928 | tf_op jit(solution)/shard_map/ppermute | solution.py:34
  78.5 311.9 %collective-permute-start.3 = (f32[2,8,135,1]{2,1,0,3:T(8,128)S(1)}, f32[2,8,135,1]{2,1,0,3:T(8,128)S(1)}, u32[]{:S(2)}, u32[]{:S(2)}) collective-permute-start(f32[2,8,135,1]{2,1,0,3:T(8,128)S(1)} %get-tuple-element.196), channel_id=1, source_target_pairs={{0,1},{1,2},{2,3},{3,4},{4,5},{5,6},{6,7},{8,9},{9,10},{10,11},{11... | collective-permute-start | bytes 25928 | tf_op jit(solution)/shard_map/ppermute | solution.py:31
  87.5 8.6 %copy-start.1 = (f32[8,135,405]{2,0,1:T(8,128)S(1)}, f32[8,135,405]{2,0,1:T(8,128)}, u32[]{:S(2)}) copy-start(f32[8,135,405]{2,0,1:T(8,128)} %param.21) | copy-start | bytes 5248804
  90.3 74.6 %collective-permute-start = (f32[2,8,1,405]{3,1,2,0:T(8,128)S(1)}, f32[2,8,1,405]{3,1,2,0:T(8,128)S(1)}, u32[]{:S(2)}, u32[]{:S(2)}) collective-permute-start(f32[2,8,1,405]{3,1,2,0:T(8,128)S(1)} %copy.51), channel_id=1, source_target_pairs={{8,0},{16,8},{24,16},{32,24},{40,32},{48,40},{56,48},{64,56},{72,6... | collective-permute-start | bytes 77768 | tf_op jit(solution)/shard_map/ppermute | solution.py:34
  96.0 71.5 %collective-permute-start.1 = (f32[2,8,1,405]{3,1,2,0:T(8,128)S(1)}, f32[2,8,1,405]{3,1,2,0:T(8,128)S(1)}, u32[]{:S(2)}, u32[]{:S(2)}) collective-permute-start(f32[2,8,1,405]{3,1,2,0:T(8,128)S(1)} %copy.53), channel_id=1, source_target_pairs={{0,8},{8,16},{16,24},{24,32},{32,40},{40,48},{48,56},{56,64},{64,7... | collective-permute-start | bytes 77768 | tf_op jit(solution)/shard_map/ppermute | solution.py:31
  103.4 24.8 %all-to-all-start = ((f32[32,2,8,135]{3,2,1,0:T(8,128)}), f32[32,2,8,135]{3,2,1,0:T(8,128)S(1)}, u32[]{:S(2)}, u32[]{:S(2)}) async-start(f32[32,2,8,135]{3,2,1,0:T(8,128)} %stack.9), calls=%async_computation | async-start | bytes 1048576 | tf_op jit(solution)/shard_map/all_to_all | solution.py:183
  113.0 9.4 %copy-start.6 = (f32[135,405]{1,0:T(8,128)S(1)}, f32[135,405]{1,0:T(8,128)}, u32[]{:S(2)}) copy-start(f32[135,405]{1,0:T(8,128)} %param.22) | copy-start | bytes 656104
  129.0 45.1 %all-to-all-start.2 = ((f32[4,2,128,144]{3,1,0,2:T(2,128)}), f32[4,2,128,144]{3,1,0,2:T(2,128)S(1)}, u32[]{:S(2)}, u32[]{:S(2)}) async-start(f32[4,2,128,144]{3,1,0,2:T(2,128)} %copy.59), calls=%async_computation.2 | async-start | bytes 2097152 | tf_op jit(solution)/shard_map/all_to_all | solution.py:165
  165.0 5.1 %copy-start.5 = (f32[32,2,8,135]{3,2,1,0:T(8,128)S(1)}, f32[32,2,8,135]{3,2,1,0:T(8,128)}, u32[]{:S(2)}) copy-start(f32[32,2,8,135]{3,2,1,0:T(8,128)} %copy-done.4) | copy-start | bytes 829444
  174.9 1.8 copy-start.7
  181.4 1.8 copy-start.7
  187.8 1.8 copy-start.7
  200.7 1.8 copy-start.7
  380.6 9.8 %copy-start.2 = (f32[2,8,1,405]{2,1,0,3:T(8,128)S(1)}, f32[2,8,1,405]{2,1,0,3:T(8,128)}, u32[]{:S(2)}) copy-start(f32[2,8,1,405]{2,1,0,3:T(8,128)} %copy.52) | copy-start | bytes 77764
  (61 other events, 79.6 us)
